TPU v7x, 256 devices: a whole 4x4x8 slice. The times are simulated.
256 devices in a mesh: plane: 2 (over core), row: 8 (over z), col: 16 (over y, x).
Axes of the slice: x: 4, y: 4, z: 8, core: 2. Of those that a mesh axis runs over, the one named last changes fastest.
Arguments:
- velocity: float32 [3, 4, 4096, 4096], P(None, 'plane', 'row', 'col'), may hold values from -60 to 60
Outputs:
- dissipation: float32 [4, 4096, 4096], P('plane', 'row', 'col')
- fine_means: float32 [128, 128], P('row', 'col')
- coarse_means: float32 [4, 4], replicated
All inputs are finite; a program needn't handle non-finite values.
Results may differ from a plain program's by a relative error of at most 0.000078.
Values sent between devices are 32-bit elements; how exact they have to be, the bound alone decides.
No kernel may reach another device: no remote copies, remote signals or barrier semaphores. Data moves between devices by JAX's collectives and lax.ppermute only.
A program may use at most 128 MiB of HBM per device.

v0:
```python
import functools
import math
import jax
import jax.numpy as jnp
from jax import lax
from jax.sharding import Mesh
from jax.sharding import PartitionSpec as P

N = 4096
FIRST = 32
FINE = 32
COARSE = 1024
PLANE_COL = ("plane", "col_0", "col_1")
COL = ("col_0", "col_1")
ROW_COL = ("row", "col_0", "col_1")
precise = lax.Precision.HIGHEST


def split_up(shard, dim, size):
    lengths = shard.shape
    blocks = shard.reshape(*lengths[:dim], size, lengths[dim] // size, *lengths[dim + 1 :])
    return jnp.moveaxis(blocks, dim, 0)


def cut_rows(length, count):
    turn = length // count
    if turn >= 8:
        turn -= turn % 8
    return [turn * k for k in range(1, count)]


def in_order(blocks, dim):
    lengths = list(blocks.shape[1:])
    lengths[dim] *= blocks.shape[0]
    return jnp.moveaxis(blocks, 0, dim).reshape(lengths)


def exchange_in_pieces(shard, axis, pieces, split_dim, concat_dim):
    blocks = split_up(shard, split_dim, lax.axis_size(axis))
    widest = max(range(1, max(2, blocks.ndim - 1)), key=lambda d: blocks.shape[d])
    outs = []
    for share in jnp.split(blocks, cut_rows(blocks.shape[widest], pieces), axis=widest):
        if share.size:
            outs.append(lax.all_to_all(share, axis, split_axis=0, concat_axis=0, tiled=True))
    return in_order(jnp.concatenate(outs, axis=widest), concat_dim)


def exchange_both(shard, axis, axes, splits, concats):
    sizes = [lax.axis_size(a) for a in axes]
    blocks = split_up(shard, splits[0], sizes[0])
    blocks = jnp.moveaxis(split_up(blocks, splits[1] + 1, sizes[1]), 0, 1)
    inside = blocks.shape[2:]
    blocks = blocks.reshape(-1, *inside)
    blocks = lax.all_to_all(blocks, axis, split_axis=0, concat_axis=0, tiled=True)
    blocks = in_order(blocks.reshape(*sizes, *inside), concats[0] + 1)
    return in_order(blocks, concats[1])


def gathered_total(shard, axis):
    return lax.all_gather(shard, axis).sum(0)


def over_axes(shard, axes):
    return functools.reduce(lax.psum, axes, shard)


def angle_table(height, across, modulus):
    left_idx = lax.broadcasted_iota(jnp.int32, (height, across), 0)
    right_idx = lax.broadcasted_iota(jnp.int32, (height, across), 1)
    turn_count = left_idx * right_idx % modulus
    phase_ang = turn_count.astype(jnp.float32) * (2.0 * math.pi / modulus)
    return (jnp.cos(phase_ang), jnp.sin(phase_ang))


def wave_table(first_len, second, length):
    low_idx = lax.broadcasted_iota(jnp.int32, (first_len, second), 0)
    high_idx = lax.broadcasted_iota(jnp.int32, (first_len, second), 1)
    indices = low_idx + first_len * high_idx
    signed = jnp.where(indices < length // 2, indices, indices - length)
    signed = jnp.where(indices == length // 2, 0, signed)
    return signed.astype(jnp.float32) * (2.0 * math.pi / length)


def left_mult(coeffs, values):
    return jnp.einsum("kn,...nm->...km", coeffs, values, precision=precise)


def right_mult(values, coeffs):
    return jnp.einsum("...kn,nm->...km", values, coeffs, precision=precise)


def derivative_last(values):
    length = values.shape[-1]
    first_len = FIRST
    second = length // first_len
    leading = values.shape[:-1]
    blocks = values.reshape(leading + (first_len, second))
    cos_a, sin_a = angle_table(first_len, first_len, first_len)
    cos_b, sin_b = angle_table(second, second, second)
    cos_t, sin_t = angle_table(first_len, second, length)
    forward_a = jnp.concatenate([cos_a, -sin_a], axis=0)
    section_a = left_mult(forward_a, blocks)
    real_a = section_a[..., :first_len, :]
    imag_a = section_a[..., first_len:, :]
    real_b = real_a * cos_t + imag_a * sin_t
    imag_b = imag_a * cos_t - real_a * sin_t
    forward_b = jnp.concatenate(
        [jnp.concatenate([cos_b, -sin_b], axis=1), jnp.concatenate([sin_b, cos_b], axis=1)], axis=0
    )
    section_c = right_mult(jnp.concatenate([real_b, imag_b], axis=-1), forward_b)
    wavenum = wave_table(first_len, second, length)
    scaled = jnp.concatenate(
        [-wavenum * section_c[..., second:], wavenum * section_c[..., :second]], axis=-1
    )
    inverse_b = jnp.concatenate(
        [jnp.concatenate([cos_b, sin_b], axis=1), jnp.concatenate([-sin_b, cos_b], axis=1)], axis=0
    )
    section_e = right_mult(scaled, inverse_b)
    real_e = section_e[..., :second]
    imag_e = section_e[..., second:]
    real_f = real_e * cos_t - imag_e * sin_t
    imag_f = real_e * sin_t + imag_e * cos_t
    inverse_a = jnp.concatenate([cos_a, -sin_a], axis=1)
    result = left_mult(inverse_a, jnp.concatenate([real_f, imag_f], axis=-2)) * (1.0 / length)
    return result.reshape(leading + (length,))


def along_rows(pencil):
    turned = jnp.swapaxes(pencil, 2, 3)
    back_turned = jnp.swapaxes(derivative_last(turned), 2, 3)
    return exchange_in_pieces(back_turned, "row", 2, 2, 3)


def per_device(velocity):
    x_local = velocity.shape[2]
    y_local = velocity.shape[3]
    plane_count = velocity.shape[1] * lax.axis_size("plane")
    grad_x = along_rows(lax.all_to_all(velocity, "row", split_axis=3, concat_axis=2, tiled=True))
    slab_data = exchange_both(velocity, PLANE_COL, ("plane", COL), (2, 2), (1, 3))
    slab_y = derivative_last(slab_data)
    slab_z = (jnp.roll(slab_data, -1, axis=1) - jnp.roll(slab_data, 1, axis=1)) * 0.5
    cross_yz = slab_z[1] + slab_y[2]
    partial_value = slab_y[1] * slab_y[1] + slab_z[2] * slab_z[2] + 0.5 * cross_yz * cross_yz
    packed = jnp.stack([partial_value, slab_y[0], slab_z[0]])
    packed = lax.all_to_all(packed, COL, split_axis=3, concat_axis=2, tiled=True)
    packed = lax.all_to_all(packed, "plane", split_axis=1, concat_axis=2, tiled=True)
    cross_xy = packed[1] + grad_x[1]
    cross_xz = packed[2] + grad_x[2]
    dissip = packed[0] + grad_x[0] * grad_x[0]
    dissip = dissip + 0.5 * (cross_xy * cross_xy + cross_xz * cross_xz)
    column_sum = jnp.sum(dissip, axis=0)
    fine_local = column_sum.reshape(x_local // FINE, FINE, y_local // FINE, FINE).sum(axis=(1, 3))
    fine_total = gathered_total(fine_local, "plane")
    fine_means = fine_total * (1.0 / (plane_count * FINE * FINE))
    local_total = jnp.sum(fine_total)
    box_count = N // COARSE
    box_row = lax.axis_index("row") * x_local // COARSE
    box_col = lax.axis_index(COL) * y_local // COARSE
    rows_hit = (lax.iota(jnp.int32, box_count) == box_row).astype(jnp.float32)
    cols_hit = (lax.iota(jnp.int32, box_count) == box_col).astype(jnp.float32)
    partial_map = rows_hit[:, None] * cols_hit[None, :] * local_total
    coarse_total = over_axes(partial_map, ROW_COL)
    coarse_means = coarse_total * (1.0 / (plane_count * COARSE * COARSE))
    return (dissip, fine_means, coarse_means)


def solution(mesh):
    split = Mesh(
        mesh.devices.reshape(mesh.shape["plane"], mesh.shape["row"], 4, 4),
        ("plane", "row", "col_0", "col_1"),
    )
    in_specs = (P(None, "plane", "row", COL),)
    out_specs = (P("plane", "row", COL), P("row", COL), P())
    return jax.shard_map(
        per_device, mesh=split, in_specs=in_specs, out_specs=out_specs, check_vma=False
    )
```

profile of v0, /device:TPU:2, one launch (start us, length us, event | category | flops | bytes accessed | tf_op | source)
XLA Modules:
  0.0 436.9 jit_solution(4735583663950403906)
XLA Ops:
  0.6 4.0 copy.91
  4.6 7.9 %all-to-all-start = ((f32[32,3,2,16,256]{4,3,2,1,0:T(8,128)}), f32[32,3,2,16,256]{4,3,2,1,0:T(8,128)}, u32[]{:S(2)}, u32[]{:S(2)}) async-start(f32[32,3,2,16,256]{4,3,2,1,0:T(8,128)} %bitcast.121), calls=%async_computation | async-start | bytes 6291456 | tf_op jit(solution)/shard_map/all_to_all | solution.py:54
  12.6 3.6 copy.102
  16.9 34.7 %all-to-all-done = f32[32,3,2,16,256]{4,3,2,1,0:T(8,128)} async-done(((f32[32,3,2,16,256]{4,3,2,1,0:T(8,128)}), f32[32,3,2,16,256]{4,3,2,1,0:T(8,128)}, u32[]{:S(2)}, u32[]{:S(2)}) %all-to-all-start) | async-done | bytes 3145760 | tf_op jit(solution)/shard_map/all_to_all | solution.py:54
  51.6 8.5 %all-to-all-start.3 = ((f32[3,2,512,256]{2,1,0,3:T(2,128)}), f32[3,2,512,256]{2,1,0,3:T(2,128)}, u32[]{:S(2)}, u32[]{:S(2)}) async-start(f32[3,2,512,256]{2,1,0,3:T(2,128)} %copy.102), calls=%async_computation.3 | async-start | bytes 6291456 | tf_op jit(solution)/shard_map/all_to_all | solution.py:138
  60.1 2.2 copy.92
  62.3 3.8 copy.93
  66.1 4.9 %reshape_reshape.3 = f32[3,4,16,32,128]{4,3,2,1,0:T(8,128)} reshape(f32[3,4,16,16,256]{4,3,2,1,0:T(8,128)} %copy.93) | data formatting | bytes 6291456 | tf_op jit(solution)/shard_map/reshape;reshape | solution.py:97
  71.0 7.3 %convolution_bitcast_fusion.1 = f32[3,4,16,64,128]{4,3,2,1,0:T(8,128)S(1)} fusion(f32[3,4,16,32,128]{4,3,2,1,0:T(8,128)} %reshape_reshape.3, f32[32,32]{0,1:T(8,128)S(1)} %get-tuple-element.40, f32[32,32]{0,1:T(8,128)S(1)} %get-tuple-element.41), kind=kOutput, calls=%fused_computation.44 | convolution fusion | flops 603981824 | bytes 9445376 | tf_op jit(solution)/shard_map/kn,...nm->...km/dot_general | solution.py:85
  79.5 5.3 %fusion = f32[3,4,16,32,256]{4,3,2,1,0:T(8,128)S(1)} fusion(f32[3,4,16,32,128]{4,3,2,1,0:T(8,128)S(1)} %get-tuple-element.15, f32[3,4,16,32,128]{4,3,2,1,0:T(8,128)S(1)} %get-tuple-element.14, f32[128,128]{1,0:T(8,128)S(1)} %get-tuple-element.45, f32[128,128]{1,0:T(8,128)S(1)} %get-tuple-element.44, f32[128,128]{1,0:T(8,128)S(1)} %fusion.47), kind=kOutput, calls=%fused_computation | convolution fusion | flops 4833607680 | bytes 12779520 | tf_op jit(solution)/shard_map/...kn,nm->...km/dot_general | solution.py:89
  85.7 5.5 %fusion.4 = f32[3,4,16,32,256]{4,3,2,1,0:T(8,128)S(1)} fusion(f32[3,4,16,32,128]{4,3,2,1,0:T(8,128)S(1)} %get-tuple-element.19, f32[3,4,16,32,128]{4,3,2,1,0:T(8,128)S(1)} %get-tuple-element.18, f32[128,128]{1,0:T(8,128)S(1)} %get-tuple-element.45, f32[128,128]{1,0:T(8,128)S(1)} %fusion.47, f32[128,128]{1,0:T(8,128)S(1)} %get-tuple-element.44), kind=kOutput, calls=%fused_computation.4 | convolution fusion | flops 4833607680 | bytes 12779520 | tf_op jit(solution)/shard_map/...kn,nm->...km/dot_general | solution.py:89
  92.3 3.8 multiply_bitcast_fusion.1
  97.8 2.4 mul.480
  100.3 2.4 squeeze.29
  102.6 2.1 copy.131
  104.7 2.6 slice.117
  112.4 16.9 %copy.96 = f32[3,4,16,4096]{2,1,0,3:T(4,128)} copy(f32[3,4,16,4096]{3,2,1,0:T(8,128)S(1)} %pad_maximum_fusion) | data formatting | bytes 6291456 | tf_op jit(solution)/shard_map/stack | solution.py:144
  129.2 23.6 %reshape.184 = f32[16,1,49152]{2,1,0:T(1,128)} reshape(f32[4096,3,4,16]{3,2,1,0:T(4,128)} %bitcast.112) | data formatting | bytes 6291456
  152.8 6.8 %all-to-all-start.1 = ((f32[16,1,49152]{2,1,0:T(1,128)}), f32[16,1,49152]{2,1,0:T(1,128)S(1)}, u32[]{:S(2)}, u32[]{:S(2)}) async-start(f32[16,1,49152]{2,1,0:T(1,128)} %reshape.184), calls=%async_computation.1 | async-start | bytes 6291456 | tf_op jit(solution)/shard_map/all_to_all | solution.py:145
  159.6 2.5 copy.103
  163.1 5.4 %convolution_bitcast_fusion = f32[3,2,32,64,128]{4,3,2,1,0:T(8,128)S(1)} fusion(f32[3,2,32,32,128]{4,3,2,1,0:T(8,128)S(1)} %bitcast.126, f32[32,32]{0,1:T(8,128)S(1)} %get-tuple-element.40, f32[32,32]{0,1:T(8,128)S(1)} %get-tuple-element.41), kind=kOutput, calls=%fused_computation.43 | convolution fusion | flops 603981824 | bytes 9445376 | tf_op jit(solution)/shard_map/kn,...nm->...km/dot_general | solution.py:85
  169.7 5.5 %fusion.12 = f32[3,2,32,32,256]{4,3,2,1,0:T(8,128)S(1)} fusion(f32[3,2,32,32,128]{4,3,2,1,0:T(8,128)S(1)} %get-tuple-element.11, f32[3,2,32,32,128]{4,3,2,1,0:T(8,128)S(1)} %get-tuple-element.10, f32[128,128]{1,0:T(8,128)S(1)} %get-tuple-element.45, f32[128,128]{1,0:T(8,128)S(1)} %get-tuple-element.44, f32[128,128]{1,0:T(8,128)S(1)} %fusion.47), kind=kOutput, calls=%fused_computation.12 | convolution fusion | flops 4833607680 | bytes 12779520 | tf_op jit(solution)/shard_map/...kn,nm->...km/dot_general | solution.py:89
  176.1 5.3 %fusion.16 = f32[3,2,32,32,256]{4,3,2,1,0:T(8,128)S(1)} fusion(f32[3,2,32,32,128]{4,3,2,1,0:T(8,128)S(1)} %get-tuple-element.17, f32[3,2,32,32,128]{4,3,2,1,0:T(8,128)S(1)} %get-tuple-element.16, f32[128,128]{1,0:T(8,128)S(1)} %get-tuple-element.45, f32[128,128]{1,0:T(8,128)S(1)} %fusion.47, f32[128,128]{1,0:T(8,128)S(1)} %get-tuple-element.44), kind=kOutput, calls=%fused_computation.16 | convolution fusion | flops 4833607680 | bytes 12779520 | tf_op jit(solution)/shard_map/...kn,nm->...km/dot_general | solution.py:89
  182.4 5.2 %multiply_bitcast_fusion = f32[3,2,32,32,128]{4,3,2,1,0:T(8,128)} fusion(f32[3,2,32,32,128]{4,3,2,1,0:T(8,128)S(1)} %get-tuple-element.9, f32[3,2,32,32,128]{4,3,2,1,0:T(8,128)S(1)} %get-tuple-element.8, f32[32,32]{0,1:T(8,128)S(1)} %get-tuple-element.40, f32[32,32]{0,1:T(8,128)S(1)} %get-tuple-element.41), kind=kOutput, calls=%fused_computation.33 | convolution fusion | flops 606341120 | bytes 9445376 | tf_op jit(solution)/shard_map/kn,...nm->...km/dot_general | solution.py:85
  187.7 4.8 %reshape.172 = f32[3,2,32,4096]{3,2,1,0:T(8,128)} reshape(f32[3,2,32,32,128]{4,3,2,1,0:T(8,128)} %multiply_bitcast_fusion) | data formatting | bytes 6291456 | tf_op jit(solution)/shard_map/reshape | solution.py:125
  192.5 4.6 %copy.134 = f32[24,8,8,512]{3,2,1,0:T(8,128)S(1)} copy(f32[24,8,8,512]{3,1,2,0:T(8,128)} %bitcast.125) | data formatting | bytes 6291456
  200.2 2.5 all-to-all-done.1
  204.9 10.1 %reduce.5 = f32[16,49152]{1,0:T(8,128)S(1)} reduce(f32[16,1,49152]{2,1,0:T(1,128)} %copy-done.2, f32[]{:T(128)} %broadcast.212), dimensions={1}, to_apply=%all_to_all.47.reduce_sub_computation | reduce | bytes 6291460 | tf_op jit(solution)/shard_map/all_to_all | solution.py:145
  215.0 27.0 %reshape.185 = f32[4096,3,4,16]{3,2,1,0:T(4,128)} reshape(f32[16,49152]{1,0:T(8,128)S(1)} %reduce.5) | data formatting | bytes 6291456
  242.0 19.5 %copy.128 = f32[3,4,16,16,256]{4,2,3,0,1:T(8,128)S(1)} copy(f32[3,4,16,16,256]{2,1,0,4,3:T(4,128)} %bitcast.113) | data formatting | bytes 6291456 | tf_op jit(solution)/shard_map/all_to_all | solution.py:145
  261.5 7.2 %all_to_all.66 = f32[3,4,256,256]{3,2,0,1:T(8,128)} all-to-all(f32[3,4,256,256]{3,2,0,1:T(8,128)S(1)} %bitcast.119), channel_id=1, replica_groups=mesh['plane'=2,'row'=8,'col_0'=4,'col_1'=4] {'plane'}, dimensions={1} | all-to-all | bytes 6291456 | tf_op jit(solution)/shard_map/all_to_all | solution.py:146
  268.8 6.2 %all-to-all-start.4 = ((f32[8,3,2,256,32]{3,4,2,1,0:T(8,128)}), f32[8,3,2,256,32]{3,4,2,1,0:T(8,128)S(1)}, u32[]{:S(2)}, u32[]{:S(2)}) async-start(f32[8,3,2,256,32]{3,4,2,1,0:T(8,128)} %copy.106), calls=%async_computation.4 | async-start | bytes 3145728 | tf_op jit(solution)/shard_map/all_to_all | solution.py:44
  276.6 38.6 %all-to-all-done.4 = f32[8,3,2,256,32]{3,4,2,1,0:T(8,128)S(1)} async-done(((f32[8,3,2,256,32]{3,4,2,1,0:T(8,128)}), f32[8,3,2,256,32]{3,4,2,1,0:T(8,128)S(1)}, u32[]{:S(2)}, u32[]{:S(2)}) %all-to-all-start.4) | async-done | bytes 1572896 | tf_op jit(solution)/shard_map/all_to_all | solution.py:44
  315.2 4.5 %all-to-all-start.5 = ((f32[8,3,2,256,32]{3,4,2,1,0:T(8,128)}), f32[8,3,2,256,32]{3,4,2,1,0:T(8,128)}, u32[]{:S(2)}, u32[]{:S(2)}) async-start(f32[8,3,2,256,32]{3,4,2,1,0:T(8,128)} %copy.107), calls=%async_computation.5 | async-start | bytes 3145728 | tf_op jit(solution)/shard_map/all_to_all | solution.py:44
  319.8 2.3 copy.100
  322.0 38.1 %all-to-all-done.5 = f32[8,3,2,256,32]{3,4,2,1,0:T(8,128)} async-done(((f32[8,3,2,256,32]{3,4,2,1,0:T(8,128)}), f32[8,3,2,256,32]{3,4,2,1,0:T(8,128)}, u32[]{:S(2)}, u32[]{:S(2)}) %all-to-all-start.5) | async-done | bytes 1572896 | tf_op jit(solution)/shard_map/all_to_all | solution.py:44
  360.1 2.3 copy_bitcast_fusion
  364.2 2.9 mul.510
  367.1 2.2 copy.115
  369.3 2.9 squeeze.35
  372.2 2.3 copy.116
  374.4 2.9 squeeze.36
  377.3 2.3 copy.117
  379.6 3.2 add_reduce_fusion
  394.9 14.7 %psum.21 = f32[4,4]{1,0:T(4,128)S(1)} all-reduce(f32[4,4]{1,0:T(4,128)S(1)} %multiply_multiply_fusion.1), channel_id=1, replica_groups=mesh['plane'=2,'row'=8,'col_0'=4,'col_1'=4] {'row'}, use_global_device_ids=true, to_apply=%region_4.5 | all-reduce | flops 16 | bytes 128 | tf_op jit(solution)/shard_map/psum | solution.py:64
  409.6 9.3 %psum.22 = f32[4,4]{1,0:T(4,128)S(1)} all-reduce(f32[4,4]{1,0:T(4,128)S(1)} %psum.21), channel_id=1, replica_groups=mesh['plane'=2,'row'=8,'col_0'=4,'col_1'=4] {'col_0'}, use_global_device_ids=true, to_apply=%region_5.6 | all-reduce | flops 16 | bytes 128 | tf_op jit(solution)/shard_map/psum | solution.py:64
  418.9 12.8 %psum.23 = f32[4,4]{1,0:T(4,128)S(1)} all-reduce(f32[4,4]{1,0:T(4,128)S(1)} %psum.22), channel_id=1, replica_groups=mesh['plane'=2,'row'=8,'col_0'=4,'col_1'=4] {'col_1'}, use_global_device_ids=true, to_apply=%region_6.7 | all-reduce | flops 16 | bytes 128 | tf_op jit(solution)/shard_map/psum | solution.py:64
  432.9 3.9 multiply_add_fusion.4
  (65 shorter events, 36.6 us)
Async XLA Ops:
  4.6 7.9 %copy-start.1 = (f32[3,2,512,256]{3,2,1,0:T(8,128)S(1)}, f32[3,2,512,256]{3,2,1,0:T(8,128)}, u32[]{:S(2)}) copy-start(f32[3,2,512,256]{3,2,1,0:T(8,128)} %param.1) | copy-start | bytes 9437188
  4.6 46.9 %all-to-all-start = ((f32[32,3,2,16,256]{4,3,2,1,0:T(8,128)}), f32[32,3,2,16,256]{4,3,2,1,0:T(8,128)}, u32[]{:S(2)}, u32[]{:S(2)}) async-start(f32[32,3,2,16,256]{4,3,2,1,0:T(8,128)} %bitcast.121), calls=%async_computation | async-start | bytes 6291456 | tf_op jit(solution)/shard_map/all_to_all | solution.py:54
  51.6 101.3 %all-to-all-start.3 = ((f32[3,2,512,256]{2,1,0,3:T(2,128)}), f32[3,2,512,256]{2,1,0,3:T(2,128)}, u32[]{:S(2)}, u32[]{:S(2)}) async-start(f32[3,2,512,256]{2,1,0,3:T(2,128)} %copy.102), calls=%async_computation.3 | async-start | bytes 6291456 | tf_op jit(solution)/shard_map/all_to_all | solution.py:138
  104.7 4.1 copy-start
  109.3 1.2 copy-start.9
  109.3 1.5 copy-start.10
  110.9 1.2 copy-start.11
  152.8 49.9 %all-to-all-start.1 = ((f32[16,1,49152]{2,1,0:T(1,128)}), f32[16,1,49152]{2,1,0:T(1,128)S(1)}, u32[]{:S(2)}, u32[]{:S(2)}) async-start(f32[16,1,49152]{2,1,0:T(1,128)} %reshape.184), calls=%async_computation.1 | async-start | bytes 6291456 | tf_op jit(solution)/shard_map/all_to_all | solution.py:145
  202.8 1.7 copy-start.2
  268.8 6.2 %copy-start.7 = (f32[8,3,2,256,32]{3,0,4,2,1:T(8,128)S(1)}, f32[8,3,2,256,32]{3,0,4,2,1:T(8,128)}, u32[]{:S(2)}) copy-start(f32[8,3,2,256,32]{3,0,4,2,1:T(8,128)} %get-tuple-element.28) | copy-start | bytes 4718596
  268.8 46.5 %all-to-all-start.4 = ((f32[8,3,2,256,32]{3,4,2,1,0:T(8,128)}), f32[8,3,2,256,32]{3,4,2,1,0:T(8,128)S(1)}, u32[]{:S(2)}, u32[]{:S(2)}) async-start(f32[8,3,2,256,32]{3,4,2,1,0:T(8,128)} %copy.106), calls=%async_computation.4 | async-start | bytes 3145728 | tf_op jit(solution)/shard_map/all_to_all | solution.py:44
  315.2 4.5 %copy-start.6 = (f32[8,3,2,256,32]{3,4,2,1,0:T(8,128)}, f32[8,3,2,256,32]{3,4,2,1,0:T(8,128)S(1)}, u32[]{:S(2)}) copy-start(f32[8,3,2,256,32]{3,4,2,1,0:T(8,128)S(1)} %all-to-all-done.4) | copy-start | bytes 4718596
  315.2 44.9 %all-to-all-start.5 = ((f32[8,3,2,256,32]{3,4,2,1,0:T(8,128)}), f32[8,3,2,256,32]{3,4,2,1,0:T(8,128)}, u32[]{:S(2)}, u32[]{:S(2)}) async-start(f32[8,3,2,256,32]{3,4,2,1,0:T(8,128)} %copy.107), calls=%async_computation.5 | async-start | bytes 3145728 | tf_op jit(solution)/shard_map/all_to_all | solution.py:44
  382.7 3.2 copy-start.5
  383.8 3.5 copy-start.4
  384.9 3.7 copy-start.3
  388.6 44.3 %copy-start.8 = (f32[1,2,2,256,256]{4,3,2,1,0:T(8,128)S(1)}, f32[1,2,2,256,256]{4,3,2,1,0:T(8,128)}, u32[]{:S(2)}) copy-start(f32[1,2,2,256,256]{4,3,2,1,0:T(8,128)} %copy.101) | copy-start | bytes 3145732
where the time goes:
time: 443 us; the launch traced here: 437 us
  local copies, waits for them, and re-layouts  165 us (37%)
  waiting for transfers between devices  114 us (26%)
  blocking collectives  45.8 us (10%)
  matrix products  43.5 us (10%)
  starting transfers between devices  33.8 us (8%)
  other arithmetic  33.5 us (8%)
    all_to_all x2, waiting for transfers between devices, exchange_in_pieces(): lax.all_to_all(share, axis, split_axis=0, concat_axis=0, tiled=True)  76.7 us
    unnamed x29, local copies, waits for them, and re-layouts  62.9 us
    psum x3, blocking collectives, over_axes(): return functools.reduce(lax.psum, axes, shard)  36.8 us
    all_to_all x1, waiting for transfers between devices, exchange_both(): lax.all_to_all(blocks, axis, split_axis=0, concat_axis=0, tiled=True)  34.7 us
    dot_general x4, matrix products, left_mult(): return jnp.einsum('kn,...nm->...km', coeffs, values, precision=precise)  21.7 us
    dot_general x4, matrix products, right_mult(): return jnp.einsum('...kn,nm->...km', values, coeffs, precision=precise)  21.7 us
    all_to_all x2, local copies, waits for them, and re-layouts, per_device(): lax.all_to_all(packed, COL, split_axis=3, concat_axis=2, tiled=True)  20 us
    another operation x1, local copies, waits for them, and re-layouts, per_device(): packed = jnp.stack([partial_value, slab_y[0], slab_z[0]])  16.9 us
  transfers between devices with their start and end apart: 5, of which 4 were waited for; matrix products, arithmetic and copies ran while one was open for 32% of the time, Pallas kernels for 0%

commit v1 on v0

--- a/solution.py
+++ b/solution.py
@@ -142,7 +142,15 @@
     cross_yz = slab_z[1] + slab_y[2]
     partial_value = slab_y[1] * slab_y[1] + slab_z[2] * slab_z[2] + 0.5 * cross_yz * cross_yz
     packed = jnp.stack([partial_value, slab_y[0], slab_z[0]])
-    packed = lax.all_to_all(packed, COL, split_axis=3, concat_axis=2, tiled=True)
+    packed = jnp.concatenate(
+        lax.all_to_all(
+            jnp.stack(jnp.split(packed, lax.axis_size(COL), axis=3), axis=0),
+            axis_name=COL,
+            split_axis=0,
+            concat_axis=0,
+        ),
+        axis=2,
+    )
     packed = lax.all_to_all(packed, "plane", split_axis=1, concat_axis=2, tiled=True)
     cross_xy = packed[1] + grad_x[1]
     cross_xz = packed[2] + grad_x[2]

time: 443 us -> 364 us (0.82)
  local copies, waits for them, and re-layouts: 165 us -> 81.2 us
  waiting for transfers between devices: 114 us -> 128 us
  other arithmetic: 33.5 us -> 27.6 us
    unnamed x29 -> x40, local copies, waits for them, and re-layouts: 62.9 us -> 17.2 us
    all_to_all x2 -> x0, local copies, waits for them, and re-layouts: 20 us -> none  [per_device(): lax.all_to_all(packed, COL, split_axis=3, concat_axis=2, tiled=True)]
    another operation x1, local copies, waits for them, and re-layouts: 16.9 us -> 0.68 us  [per_device(): jnp.stack(jnp.split(packed, lax.axis_size(COL), axis=3), axis=0)]
    all_to_all x1 -> x0, other arithmetic: 10.1 us -> none  [per_device(): lax.all_to_all(packed, COL, split_axis=3, concat_axis=2, tiled=True)]
    all_to_all x1, waiting for transfers between devices: 2.54 us -> 10.4 us  [per_device(): lax.all_to_all(jnp.stack(jnp.split(packed, lax.axis_size(COL), axis=3), a...]
    all_to_all x1, waiting for transfers between devices: 0.01 us -> 7.83 us  [per_device(): lax.all_to_all(velocity, 'row', split_axis=3, concat_axis=2, tiled=True)]
  transfers between devices with their start and end apart: 5 -> 5, of which waited for: 4 -> 5; matrix products, arithmetic and copies ran while one was open for 32% -> 30% of each run, Pallas kernels for 0% -> 0%
where the time goes in v1:
time: 364 us; the launch traced here: 358 us
  waiting for transfers between devices  128 us (35%)
  local copies, waits for them, and re-layouts  81.2 us (22%)
  blocking collectives  45.5 us (12%)
  matrix products  43.7 us (12%)
  starting transfers between devices  31.4 us (9%)
  other arithmetic  27.6 us (8%)
    all_to_all x2, waiting for transfers between devices, exchange_in_pieces(): lax.all_to_all(share, axis, split_axis=0, concat_axis=0, tiled=True)  74.7 us
    psum x3, blocking collectives, over_axes(): return functools.reduce(lax.psum, axes, shard)  36.4 us
    all_to_all x1, waiting for transfers between devices, exchange_both(): lax.all_to_all(blocks, axis, split_axis=0, concat_axis=0, tiled=True)  34.7 us
    dot_general x4, matrix products, right_mult(): return jnp.einsum('...kn,nm->...km', values, coeffs, precision=precise)  22 us
    dot_general x4, matrix products, left_mult(): return jnp.einsum('kn,...nm->...km', coeffs, values, precision=precise)  21.7 us
    unnamed x40, local copies, waits for them, and re-layouts  17.2 us
    all_to_all x1, waiting for transfers between devices, per_device(): lax.all_to_all(jnp.stack(jnp.split(packed, lax.axis_size(COL), axis=3), a...  10.4 us
    all_to_all x1, starting transfers between devices, per_device(): lax.all_to_all(velocity, 'row', split_axis=3, concat_axis=2, tiled=True)  8.47 us
  transfers between devices with their start and end apart: 5, of which 5 were waited for; matrix products, arithmetic and copies ran while one was open for 30% of the time, Pallas kernels for 0%

profile of v1, /device:TPU:2, one launch (start us, length us, event | category | flops | bytes accessed | tf_op | source)
XLA Modules:
  0.0 358.4 jit_solution(1505324255066678966)
XLA Ops:
  0.6 4.0 %copy.118 = f32[2,16,3,2,16,256]{5,4,3,2,1,0:T(8,128)} copy(f32[2,16,3,2,16,256]{5,4,1,0,3,2:T(8,128)} %bitcast.176) | data formatting | bytes 6291456 | tf_op jit(solution)/shard_map/transpose;transpose | solution.py:51
  4.7 7.9 %all-to-all-start = ((f32[32,3,2,16,256]{4,3,2,1,0:T(8,128)}), f32[32,3,2,16,256]{4,3,2,1,0:T(8,128)}, u32[]{:S(2)}, u32[]{:S(2)}) async-start(f32[32,3,2,16,256]{4,3,2,1,0:T(8,128)} %bitcast.177), calls=%async_computation | async-start | bytes 6291456 | tf_op jit(solution)/shard_map/all_to_all | solution.py:54
  12.6 3.5 copy.127
  16.9 34.7 %all-to-all-done = f32[32,3,2,16,256]{4,3,2,1,0:T(8,128)} async-done(((f32[32,3,2,16,256]{4,3,2,1,0:T(8,128)}), f32[32,3,2,16,256]{4,3,2,1,0:T(8,128)}, u32[]{:S(2)}, u32[]{:S(2)}) %all-to-all-start) | async-done | bytes 3145760 | tf_op jit(solution)/shard_map/all_to_all | solution.py:54
  51.6 8.5 %all-to-all-start.3 = ((f32[3,2,512,256]{2,1,0,3:T(2,128)}), f32[3,2,512,256]{2,1,0,3:T(2,128)S(1)}, u32[]{:S(2)}, u32[]{:S(2)}) async-start(f32[3,2,512,256]{2,1,0,3:T(2,128)} %copy.127), calls=%async_computation.3 | async-start | bytes 6291456 | tf_op jit(solution)/shard_map/all_to_all | solution.py:138
  60.1 2.4 copy.119
  63.0 2.8 fusion.95
  67.0 3.9 %copy.120 = f32[3,4,16,16,256]{4,3,2,1,0:T(8,128)} copy(f32[3,4,16,16,256]{4,2,1,0,3:T(8,128)S(1)} %bitcast.172) | data formatting | bytes 6291456 | tf_op jit(solution)/shard_map/transpose | solution.py:35
  70.9 4.7 %reshape_reshape.3 = f32[3,4,16,32,128]{4,3,2,1,0:T(8,128)} reshape(f32[3,4,16,16,256]{4,3,2,1,0:T(8,128)} %copy.120) | data formatting | bytes 6291456 | tf_op jit(solution)/shard_map/reshape;reshape | solution.py:97
  75.5 7.3 %convolution_bitcast_fusion.1 = f32[3,4,16,64,128]{4,3,2,1,0:T(8,128)S(1)} fusion(f32[3,4,16,32,128]{4,3,2,1,0:T(8,128)} %reshape_reshape.3, f32[32,32]{0,1:T(8,128)S(1)} %get-tuple-element.40, f32[32,32]{0,1:T(8,128)S(1)} %get-tuple-element.41), kind=kOutput, calls=%fused_computation.44 | convolution fusion | flops 603981824 | bytes 9445376 | tf_op jit(solution)/shard_map/kn,...nm->...km/dot_general | solution.py:85
  84.0 5.3 %fusion = f32[3,4,16,32,256]{4,3,2,1,0:T(8,128)S(1)} fusion(f32[3,4,16,32,128]{4,3,2,1,0:T(8,128)S(1)} %get-tuple-element.15, f32[3,4,16,32,128]{4,3,2,1,0:T(8,128)S(1)} %get-tuple-element.14, f32[128,128]{1,0:T(8,128)S(1)} %get-tuple-element.45, f32[128,128]{1,0:T(8,128)S(1)} %get-tuple-element.44, f32[128,128]{1,0:T(8,128)S(1)} %fusion.63), kind=kOutput, calls=%fused_computation | convolution fusion | flops 4833607680 | bytes 12779520 | tf_op jit(solution)/shard_map/...kn,nm->...km/dot_general | solution.py:89
  90.3 5.8 %fusion.4 = f32[3,4,16,32,256]{4,3,2,1,0:T(8,128)S(1)} fusion(f32[3,4,16,32,128]{4,3,2,1,0:T(8,128)S(1)} %get-tuple-element.19, f32[3,4,16,32,128]{4,3,2,1,0:T(8,128)S(1)} %get-tuple-element.18, f32[128,128]{1,0:T(8,128)S(1)} %get-tuple-element.45, f32[128,128]{1,0:T(8,128)S(1)} %fusion.63, f32[128,128]{1,0:T(8,128)S(1)} %get-tuple-element.44), kind=kOutput, calls=%fused_computation.4 | convolution fusion | flops 4833607680 | bytes 12779520 | tf_op jit(solution)/shard_map/...kn,nm->...km/dot_general | solution.py:89
  97.1 3.7 %multiply_bitcast_fusion.1 = f32[3,4,16,32,128]{4,3,2,1,0:T(8,128)S(1)} fusion(f32[3,4,16,32,128]{4,3,2,1,0:T(8,128)S(1)} %get-tuple-element.13, f32[3,4,16,32,128]{4,3,2,1,0:T(8,128)S(1)} %get-tuple-element.12, f32[32,32]{0,1:T(8,128)S(1)} %get-tuple-element.40, f32[32,32]{0,1:T(8,128)S(1)} %get-tuple-element.41), kind=kOutput, calls=%fused_computation.38 | convolution fusion | flops 606341120 | bytes 9445376 | tf_op jit(solution)/shard_map/kn,...nm->...km/dot_general | solution.py:85
  100.8 2.1 fusion.24
  104.6 2.4 mul.480
  107.0 2.4 squeeze.29
  109.4 2.5 slice.117
  111.9 2.9 fusion.29
  126.2 7.8 %all-to-all-done.3 = f32[3,2,512,256]{2,1,0,3:T(2,128)S(1)} async-done(((f32[3,2,512,256]{2,1,0,3:T(2,128)}), f32[3,2,512,256]{2,1,0,3:T(2,128)S(1)}, u32[]{:S(2)}, u32[]{:S(2)}) %all-to-all-start.3) | async-done | bytes 3145760 | tf_op jit(solution)/shard_map/all_to_all | solution.py:138
  134.1 7.1 %all-to-all-start.1 = ((f32[16,3,4,16,256]{4,3,2,1,0:T(8,128)}), f32[16,3,4,16,256]{4,3,2,1,0:T(8,128)}, u32[]{:S(2)}, u32[]{:S(2)}) async-start(f32[16,3,4,16,256]{4,3,2,1,0:T(8,128)} %fusion.39), calls=%async_computation.1 | async-start | bytes 6291456 | tf_op jit(solution)/shard_map/all_to_all | solution.py:146
  142.7 5.4 %convolution_bitcast_fusion = f32[3,2,32,64,128]{4,3,2,1,0:T(8,128)S(1)} fusion(f32[3,2,32,32,128]{4,3,2,1,0:T(8,128)S(1)} %bitcast.183, f32[32,32]{0,1:T(8,128)S(1)} %get-tuple-element.40, f32[32,32]{0,1:T(8,128)S(1)} %get-tuple-element.41), kind=kOutput, calls=%fused_computation.43 | convolution fusion | flops 603981824 | bytes 9445376 | tf_op jit(solution)/shard_map/kn,...nm->...km/dot_general | solution.py:85
  149.3 5.6 %fusion.12 = f32[3,2,32,32,256]{4,3,2,1,0:T(8,128)S(1)} fusion(f32[3,2,32,32,128]{4,3,2,1,0:T(8,128)S(1)} %get-tuple-element.11, f32[3,2,32,32,128]{4,3,2,1,0:T(8,128)S(1)} %get-tuple-element.10, f32[128,128]{1,0:T(8,128)S(1)} %get-tuple-element.45, f32[128,128]{1,0:T(8,128)S(1)} %get-tuple-element.44, f32[128,128]{1,0:T(8,128)S(1)} %fusion.63), kind=kOutput, calls=%fused_computation.12 | convolution fusion | flops 4833607680 | bytes 12779520 | tf_op jit(solution)/shard_map/...kn,nm->...km/dot_general | solution.py:89
  155.8 5.3 %fusion.16 = f32[3,2,32,32,256]{4,3,2,1,0:T(8,128)S(1)} fusion(f32[3,2,32,32,128]{4,3,2,1,0:T(8,128)S(1)} %get-tuple-element.17, f32[3,2,32,32,128]{4,3,2,1,0:T(8,128)S(1)} %get-tuple-element.16, f32[128,128]{1,0:T(8,128)S(1)} %get-tuple-element.45, f32[128,128]{1,0:T(8,128)S(1)} %fusion.63, f32[128,128]{1,0:T(8,128)S(1)} %get-tuple-element.44), kind=kOutput, calls=%fused_computation.16 | convolution fusion | flops 4833607680 | bytes 12779520 | tf_op jit(solution)/shard_map/...kn,nm->...km/dot_general | solution.py:89
  162.1 5.3 %multiply_bitcast_fusion = f32[3,2,32,32,128]{4,3,2,1,0:T(8,128)} fusion(f32[3,2,32,32,128]{4,3,2,1,0:T(8,128)S(1)} %get-tuple-element.9, f32[3,2,32,32,128]{4,3,2,1,0:T(8,128)S(1)} %get-tuple-element.8, f32[32,32]{0,1:T(8,128)S(1)} %get-tuple-element.40, f32[32,32]{0,1:T(8,128)S(1)} %get-tuple-element.41), kind=kOutput, calls=%fused_computation.33 | convolution fusion | flops 606341120 | bytes 9445376 | tf_op jit(solution)/shard_map/kn,...nm->...km/dot_general | solution.py:85
  167.4 3.1 reshape.180
  170.5 2.7 copy.156
  175.2 10.4 %all-to-all-done.1 = f32[16,3,4,16,256]{4,3,2,1,0:T(8,128)} async-done(((f32[16,3,4,16,256]{4,3,2,1,0:T(8,128)}), f32[16,3,4,16,256]{4,3,2,1,0:T(8,128)}, u32[]{:S(2)}, u32[]{:S(2)}) %all-to-all-start.1) | async-done | bytes 3145760 | tf_op jit(solution)/shard_map/all_to_all | solution.py:146
  185.5 2.2 copy.123
  188.0 7.3 %all_to_all.53 = f32[3,4,256,256]{3,2,0,1:T(8,128)} all-to-all(f32[3,4,256,256]{3,2,0,1:T(8,128)S(1)} %copy.124), channel_id=1, replica_groups=mesh['plane'=2,'row'=8,'col_0'=4,'col_1'=4] {'plane'}, dimensions={1} | all-to-all | bytes 6291456 | tf_op jit(solution)/shard_map/all_to_all | solution.py:154
  195.2 3.6 all-to-all-start.4
  200.5 38.8 %all-to-all-done.4 = f32[8,3,2,256,32]{3,4,2,1,0:T(8,128)S(1)} async-done(((f32[8,3,2,256,32]{3,4,2,1,0:T(8,128)}), f32[8,3,2,256,32]{3,4,2,1,0:T(8,128)S(1)}, u32[]{:S(2)}, u32[]{:S(2)}) %all-to-all-start.4) | async-done | bytes 1572896 | tf_op jit(solution)/shard_map/all_to_all | solution.py:44
  239.3 4.3 %all-to-all-start.5 = ((f32[8,3,2,256,32]{3,4,2,1,0:T(8,128)}), f32[8,3,2,256,32]{3,4,2,1,0:T(8,128)}, u32[]{:S(2)}, u32[]{:S(2)}) async-start(f32[8,3,2,256,32]{3,4,2,1,0:T(8,128)} %copy.132), calls=%async_computation.5 | async-start | bytes 3145728 | tf_op jit(solution)/shard_map/all_to_all | solution.py:44
  243.7 2.3 copy.125
  245.9 35.9 %all-to-all-done.5 = f32[8,3,2,256,32]{3,4,2,1,0:T(8,128)} async-done(((f32[8,3,2,256,32]{3,4,2,1,0:T(8,128)}), f32[8,3,2,256,32]{3,4,2,1,0:T(8,128)}, u32[]{:S(2)}, u32[]{:S(2)}) %all-to-all-start.5) | async-done | bytes 1572896 | tf_op jit(solution)/shard_map/all_to_all | solution.py:44
  281.9 2.3 copy_bitcast_fusion
  284.1 1.8 slice_multiply_fusion.4
  285.9 2.9 mul.510
  288.8 2.2 copy.140
  291.0 2.8 squeeze.35
  293.9 2.2 copy.141
  296.1 2.9 squeeze.36
  299.0 2.3 copy.142
  301.2 3.2 add_reduce_fusion
  313.4 1.8 all-gather.1
  316.5 14.7 %psum.21 = f32[4,4]{1,0:T(4,128)S(1)} all-reduce(f32[4,4]{1,0:T(4,128)S(1)} %multiply_multiply_fusion.1), channel_id=1, replica_groups=mesh['plane'=2,'row'=8,'col_0'=4,'col_1'=4] {'row'}, use_global_device_ids=true, to_apply=%region_4.5 | all-reduce | flops 16 | bytes 128 | tf_op jit(solution)/shard_map/psum | solution.py:64
  331.2 9.7 %psum.22 = f32[4,4]{1,0:T(4,128)S(1)} all-reduce(f32[4,4]{1,0:T(4,128)S(1)} %psum.21), channel_id=1, replica_groups=mesh['plane'=2,'row'=8,'col_0'=4,'col_1'=4] {'col_0'}, use_global_device_ids=true, to_apply=%region_5.6 | all-reduce | flops 16 | bytes 128 | tf_op jit(solution)/shard_map/psum | solution.py:64
  341.0 12.0 %psum.23 = f32[4,4]{1,0:T(4,128)S(1)} all-reduce(f32[4,4]{1,0:T(4,128)S(1)} %psum.22), channel_id=1, replica_groups=mesh['plane'=2,'row'=8,'col_0'=4,'col_1'=4] {'col_1'}, use_global_device_ids=true, to_apply=%region_6.7 | all-reduce | flops 16 | bytes 128 | tf_op jit(solution)/shard_map/psum | solution.py:64
  354.1 3.9 %multiply_add_fusion.4 = f32[2,512,256]{2,1,0:T(8,128)} fusion(f32[2,512,256]{2,1,0:T(8,128)} %bitcast.189, f32[2,512,256]{2,1,0:T(8,128)} %copy.139, f32[2,512,256]{2,1,0:T(8,128)} %bitcast.188, f32[2,512,256]{2,1,0:T(8,128)} %copy.137, f32[2,512,256]{2,1,0:T(8,128)S(1)} %bitcast.187, f32[2,512,256]{2,1,0:T(8,128)} %copy.135), kind=kLoop, calls=%fused_computation.53 | loop fusion | flops 2097152 | bytes 7340032 | tf_op jit(solution)/shard_map/add | solution.py:158
  (75 shorter events, 38.4 us)
Async XLA Ops:
  4.7 7.9 %copy-start = (f32[3,2,512,256]{3,2,1,0:T(8,128)S(1)}, f32[3,2,512,256]{3,2,1,0:T(8,128)}, u32[]{:S(2)}) copy-start(f32[3,2,512,256]{3,2,1,0:T(8,128)} %param.1) | copy-start | bytes 9437188
  4.7 46.9 %all-to-all-start = ((f32[32,3,2,16,256]{4,3,2,1,0:T(8,128)}), f32[32,3,2,16,256]{4,3,2,1,0:T(8,128)}, u32[]{:S(2)}, u32[]{:S(2)}) async-start(f32[32,3,2,16,256]{4,3,2,1,0:T(8,128)} %bitcast.177), calls=%async_computation | async-start | bytes 6291456 | tf_op jit(solution)/shard_map/all_to_all | solution.py:54
  51.6 82.4 %all-to-all-start.3 = ((f32[3,2,512,256]{2,1,0,3:T(2,128)}), f32[3,2,512,256]{2,1,0,3:T(2,128)S(1)}, u32[]{:S(2)}, u32[]{:S(2)}) async-start(f32[3,2,512,256]{2,1,0,3:T(2,128)} %copy.127), calls=%async_computation.3 | async-start | bytes 6291456 | tf_op jit(solution)/shard_map/all_to_all | solution.py:138
  97.0 3.8 %copy-start.4 = (f32[3,3,16,4096]{3,2,1,0:T(8,128)S(1)}, f32[3,3,16,4096]{3,2,1,0:T(8,128)}, u32[]{:S(2)}) copy-start(f32[3,3,16,4096]{3,2,1,0:T(8,128)} %get-tuple-element.36) | copy-start | bytes 7077892
  97.0 3.8 %copy-start.5 = (f32[3,3,16,4096]{3,2,1,0:T(8,128)S(1)}, f32[3,3,16,4096]{3,2,1,0:T(8,128)}, u32[]{:S(2)}) copy-start(f32[3,3,16,4096]{3,2,1,0:T(8,128)} %get-tuple-element.37) | copy-start | bytes 7077892
  97.0 3.8 %copy-start.9 = (f32[3,1,16,4096]{3,2,1,0:T(8,128)S(1)}, f32[3,1,16,4096]{3,2,1,0:T(8,128)}, u32[]{:S(2)}) copy-start(f32[3,1,16,4096]{3,2,1,0:T(8,128)} %get-tuple-element.34) | copy-start | bytes 2359300
  97.0 3.8 %copy-start.10 = (f32[3,1,16,4096]{3,2,1,0:T(8,128)S(1)}, f32[3,1,16,4096]{3,2,1,0:T(8,128)}, u32[]{:S(2)}) copy-start(f32[3,1,16,4096]{3,2,1,0:T(8,128)} %get-tuple-element.35) | copy-start | bytes 2359300
  111.9 2.9 copy-start.8
  134.1 51.5 %all-to-all-start.1 = ((f32[16,3,4,16,256]{4,3,2,1,0:T(8,128)}), f32[16,3,4,16,256]{4,3,2,1,0:T(8,128)}, u32[]{:S(2)}, u32[]{:S(2)}) async-start(f32[16,3,4,16,256]{4,3,2,1,0:T(8,128)} %fusion.39), calls=%async_computation.1 | async-start | bytes 6291456 | tf_op jit(solution)/shard_map/all_to_all | solution.py:146
  195.2 44.0 %all-to-all-start.4 = ((f32[8,3,2,256,32]{3,4,2,1,0:T(8,128)}), f32[8,3,2,256,32]{3,4,2,1,0:T(8,128)S(1)}, u32[]{:S(2)}, u32[]{:S(2)}) async-start(f32[8,3,2,256,32]{3,4,2,1,0:T(8,128)} %copy.131), calls=%async_computation.4 | async-start | bytes 3145728 | tf_op jit(solution)/shard_map/all_to_all | solution.py:44
  239.3 4.3 %copy-start.6 = (f32[8,3,2,256,32]{3,4,2,1,0:T(8,128)}, f32[8,3,2,256,32]{3,4,2,1,0:T(8,128)S(1)}, u32[]{:S(2)}) copy-start(f32[8,3,2,256,32]{3,4,2,1,0:T(8,128)S(1)} %all-to-all-done.4) | copy-start | bytes 4718596
  239.3 42.6 %all-to-all-start.5 = ((f32[8,3,2,256,32]{3,4,2,1,0:T(8,128)}), f32[8,3,2,256,32]{3,4,2,1,0:T(8,128)}, u32[]{:S(2)}, u32[]{:S(2)}) async-start(f32[8,3,2,256,32]{3,4,2,1,0:T(8,128)} %copy.132), calls=%async_computation.5 | async-start | bytes 3145728 | tf_op jit(solution)/shard_map/all_to_all | solution.py:44
  304.4 3.1 copy-start.3
  305.4 3.5 copy-start.2
  306.5 3.7 %copy-start.1 = (f32[1,2,512,8,32]{2,4,3,1,0:T(8,128)S(1)}, f32[1,2,512,8,32]{2,4,3,1,0:T(8,128)}, u32[]{:S(2)}) copy-start(f32[1,2,512,8,32]{2,4,3,1,0:T(8,128)} %get-tuple-element.25) | copy-start | bytes 3145732
  310.2 43.9 %copy-start.7 = (f32[1,2,2,256,256]{4,3,2,1,0:T(8,128)S(1)}, f32[1,2,2,256,256]{4,3,2,1,0:T(8,128)}, u32[]{:S(2)}) copy-start(f32[1,2,2,256,256]{4,3,2,1,0:T(8,128)} %copy.126) | copy-start | bytes 3145732
